TPU v7x, 32 devices: a whole 2x2x4 slice. The times are simulated.
32 devices in a mesh: seq: 8 (over z, y), head: 4 (over x, core).
Axes of the slice: x: 2, y: 2, z: 4, core: 2. Of those that a mesh axis runs over, the one named last changes fastest.
Arguments:
- queries: bfloat16 [8192, 512], P(('seq', 'head')), may hold values from -6 to 6
- key_rows: bfloat16 [8192, 128], P(('seq', 'head')), may hold values from -6 to 6
- value_rows: bfloat16 [8192, 128], P(('seq', 'head')), may hold values from -6 to 6
- out_grad: bfloat16 [8192, 512], P(('seq', 'head')), may hold values from -6 to 6
- doc_start: int32 [32], replicated, may hold values from 0 to 255
Outputs:
- outputs: bfloat16 [8192, 512], P(('seq', 'head'))
- query_grad: bfloat16 [8192, 512], P(('seq', 'head'))
- key_grad: bfloat16 [8192, 128], P(('seq', 'head'))
- value_grad: bfloat16 [8192, 128], P(('seq', 'head'))
Inputs may be any that keep to these rules, and one draw needn't show every extreme that they name: doc_start[c] is the position within span c of the first token of a new document.
All inputs are finite; a program needn't handle non-finite values.
Results may differ from a plain program's by a relative error of at most 0.0065.
Values may be sent and summed in bfloat16 or wider, within the bound.
No kernel may reach another device: no remote copies, remote signals or barrier semaphores. Data moves between devices by JAX's collectives and lax.ppermute only.
A program may use at most 128 MiB of HBM per device.

v0:
```python
import math
import jax
import jax.numpy as jnp
from jax import lax
from jax.sharding import PartitionSpec as P

HD = 128
GROUP = 4
SPANS_DEV = 4
masked_fill = -1e30


def passed_along(value, axis, steps):
    count = lax.axis_size(axis)
    first, last = (max(0, -steps), min(count, count - steps))
    return lax.ppermute(value, axis, [(source, source + steps) for source in range(first, last)])


def allowed_mask(
    first_row, row_count, key_count, halo_len, span_len, span_start, prev_begin, span_index
):
    row_pos = first_row + lax.broadcasted_iota(jnp.int32, (row_count, key_count), 0)
    col_pos = lax.broadcasted_iota(jnp.int32, (row_count, key_count), 1) - halo_len
    return (
        (col_pos <= row_pos)
        & ((col_pos >= span_start) | (span_start > row_pos))
        & (col_pos >= prev_begin - span_len)
        & ((col_pos >= 0) | (span_index > 0))
    )


def attend(query_rows, grad_rows, key_block, value_block, allowed, head_dim):
    score_scale = 1.0 / math.sqrt(head_dim)
    contract = (((2,), (2,)), ((0,), (0,)))
    forward = (((2,), (1,)), ((0,), (0,)))
    backward = (((1,), (1,)), ((0,), (0,)))
    scores = (
        lax.dot_general(query_rows, key_block, contract, preferred_element_type=jnp.float32)
        * score_scale
    )
    masked = jnp.where(allowed, scores, masked_fill)
    row_max = jnp.max(masked, axis=2, keepdims=True)
    exp_scores = jnp.where(allowed, jnp.exp(masked - row_max), 0.0)
    weights = exp_scores / jnp.sum(exp_scores, axis=2, keepdims=True)
    weights_low = weights.astype(jnp.bfloat16)
    result = lax.dot_general(
        weights_low, value_block, forward, preferred_element_type=jnp.float32
    ).astype(jnp.bfloat16)
    grad_weights = lax.dot_general(
        grad_rows, value_block, contract, preferred_element_type=jnp.float32
    )
    row_delta = jnp.sum(weights * grad_weights, axis=2, keepdims=True)
    grad_scores = (weights * (grad_weights - row_delta) * score_scale).astype(jnp.bfloat16)
    grad_query = lax.dot_general(
        grad_scores, key_block, forward, preferred_element_type=jnp.float32
    )
    grad_key = lax.dot_general(
        grad_scores, query_rows, backward, preferred_element_type=jnp.float32
    )
    grad_value = lax.dot_general(
        weights_low, grad_rows, backward, preferred_element_type=jnp.float32
    )
    return (result, grad_query, grad_key, grad_value)


def per_device(queries, key_rows, value_rows, out_grad, doc_start):
    tok_count = queries.shape[0]
    head_count = lax.axis_size("head")
    group_rows = tok_count * head_count
    span_len = group_rows // SPANS_DEV
    halo_len = span_len // 4
    half_len = span_len // 2
    rest_len = span_len - halo_len
    head_q, head_grad = (
        lax.all_to_all(queries, "head", split_axis=1, concat_axis=0, tiled=True),
        lax.all_to_all(out_grad, "head", split_axis=1, concat_axis=0, tiled=True),
    )
    full_k, full_v = (
        lax.all_gather(key_rows, "head", axis=0, tiled=True),
        lax.all_gather(value_rows, "head", axis=0, tiled=True),
    )
    column = lax.axis_index("head") // GROUP * HD
    head_k = lax.dynamic_slice_in_dim(full_k, column, HD, 1)
    head_v = lax.dynamic_slice_in_dim(full_v, column, HD, 1)
    query_3 = head_q.reshape(SPANS_DEV, span_len, HD)
    grad_3 = head_grad.reshape(SPANS_DEV, span_len, HD)
    keys_3 = head_k.reshape(SPANS_DEV, span_len, HD)
    values_3 = head_v.reshape(SPANS_DEV, span_len, HD)
    tail_k = keys_3[:, rest_len:]
    tail_v = values_3[:, rest_len:]
    edge_last_k, edge_last_v = passed_along(
        (tail_k[SPANS_DEV - 1], tail_v[SPANS_DEV - 1]), "seq", 1
    )
    edge_k = jnp.concatenate([edge_last_k[None], tail_k[: SPANS_DEV - 1]], axis=0)
    edge_v = jnp.concatenate([edge_last_v[None], tail_v[: SPANS_DEV - 1]], axis=0)
    key_block = jnp.concatenate([edge_k, keys_3], axis=1)
    value_block = jnp.concatenate([edge_v, values_3], axis=1)
    first_span = lax.axis_index("seq") * SPANS_DEV
    span_starts = lax.dynamic_slice_in_dim(doc_start, first_span, SPANS_DEV)
    before_start = lax.dynamic_slice_in_dim(doc_start, jnp.maximum(first_span - 1, 0), 1)
    prev_starts = jnp.concatenate([before_start, span_starts[: SPANS_DEV - 1]], axis=0)
    span_ids = first_span + jnp.arange(SPANS_DEV, dtype=jnp.int32)
    span_starts = span_starts.reshape(SPANS_DEV, 1, 1)
    prev_starts = prev_starts.reshape(SPANS_DEV, 1, 1)
    span_ids = span_ids.reshape(SPANS_DEV, 1, 1)
    grad_key = jnp.zeros((SPANS_DEV, halo_len + span_len, HD), jnp.float32)
    grad_value = jnp.zeros((SPANS_DEV, halo_len + span_len, HD), jnp.float32)
    results = []
    query_grads = []
    for block_index in range(2):
        first_row = block_index * half_len
        key_count = halo_len + first_row + half_len
        allowed = allowed_mask(
            first_row, half_len, key_count, halo_len, span_len, span_starts, prev_starts, span_ids
        )
        result, grad_query, part_key, part_value = attend(
            query_3[:, first_row : first_row + half_len],
            grad_3[:, first_row : first_row + half_len],
            key_block[:, :key_count],
            value_block[:, :key_count],
            allowed,
            HD,
        )
        results.append(result)
        query_grads.append(grad_query.astype(jnp.bfloat16))
        grad_key = grad_key.at[:, :key_count].add(part_key)
        grad_value = grad_value.at[:, :key_count].add(part_value)
    next_last_k, next_last_v = passed_along(
        (grad_key[0, :halo_len], grad_value[0, :halo_len]), "seq", -1
    )
    next_k = jnp.concatenate([grad_key[1:, :halo_len], next_last_k[None]], axis=0)
    next_v = jnp.concatenate([grad_value[1:, :halo_len], next_last_v[None]], axis=0)
    own_k = jnp.concatenate(
        [grad_key[:, halo_len : halo_len + rest_len], grad_key[:, halo_len + rest_len :] + next_k],
        axis=1,
    ).reshape(group_rows, HD)
    own_v = jnp.concatenate(
        [
            grad_value[:, halo_len : halo_len + rest_len],
            grad_value[:, halo_len + rest_len :] + next_v,
        ],
        axis=1,
    ).reshape(group_rows, HD)
    all_results = jnp.concatenate(results, axis=1).reshape(group_rows, HD)
    all_query_grads = jnp.concatenate(query_grads, axis=1).reshape(group_rows, HD)
    outputs, query_grad = (
        lax.all_to_all(all_results, "head", split_axis=0, concat_axis=1, tiled=True),
        lax.all_to_all(all_query_grads, "head", split_axis=0, concat_axis=1, tiled=True),
    )
    wide_gk, wide_gv = (
        lax.all_to_all(own_k, "head", split_axis=0, concat_axis=1, tiled=True),
        lax.all_to_all(own_v, "head", split_axis=0, concat_axis=1, tiled=True),
    )
    group_total = wide_gk.shape[1] // (GROUP * HD)
    key_grad = (
        wide_gk.reshape(tok_count, group_total, GROUP, HD)
        .sum(axis=2)
        .reshape(tok_count, group_total * HD)
        .astype(jnp.bfloat16)
    )
    value_grad = (
        wide_gv.reshape(tok_count, group_total, GROUP, HD)
        .sum(axis=2)
        .reshape(tok_count, group_total * HD)
        .astype(jnp.bfloat16)
    )
    return (outputs, query_grad, key_grad, value_grad)


def solution(mesh):
    placed = (
        P(("seq", "head"), None),
        P(("seq", "head"), None),
        P(("seq", "head"), None),
        P(("seq", "head"), None),
        P(),
    )
    return jax.shard_map(
        per_device,
        mesh=mesh,
        in_specs=placed,
        out_specs=(
            P(("seq", "head"), None),
            P(("seq", "head"), None),
            P(("seq", "head"), None),
            P(("seq", "head"), None),
        ),
        check_vma=False,
    )
```

profile of v0, /device:TPU:8, one launch (start us, length us, event | category | flops | bytes accessed | tf_op | source)
XLA Modules:
  0.0 94.2 jit_solution(2533710951645964501)
XLA Ops:
  0.6 6.1 %all_gather.7 = bf16[1024,128]{1,0:T(8,128)(2,1)S(1)} all-gather(bf16[256,128]{1,0:T(8,128)(2,1)} %param.19), channel_id=1, replica_groups=mesh['seq'=8,'head'=4] {'head'}, dimensions={0}, use_global_device_ids=true | all-gather | bytes 327680 | tf_op jit(solution)/shard_map/all_gather | solution.py:80
  6.8 3.5 %collective-permute-start.1 = (bf16[64,128]{1,0:T(8,128)(2,1)S(1)}, bf16[64,128]{1,0:T(8,128)(2,1)S(1)}, u32[]{:S(2)}, u32[]{:S(2)}) collective-permute-start(bf16[64,128]{1,0:T(8,128)(2,1)S(1)} %slice_bitcast_fusion.2), channel_id=1, source_target_pairs={{0,4},{4,8},{8,12},{12,16},{16,20},{20,24},{24,28},{1,5},{5,9},{9,... | collective-permute-start | bytes 49160 | tf_op jit(solution)/shard_map/ppermute | solution.py:16
  10.3 5.8 %all_gather.6 = bf16[1024,128]{1,0:T(8,128)(2,1)S(1)} all-gather(bf16[256,128]{1,0:T(8,128)(2,1)S(1)} %copy-done.2), channel_id=1, replica_groups=mesh['seq'=8,'head'=4] {'head'}, dimensions={0}, use_global_device_ids=true | all-gather | bytes 327680 | tf_op jit(solution)/shard_map/all_gather | solution.py:79
  16.1 3.4 %collective-permute-start = (bf16[64,128]{1,0:T(8,128)(2,1)S(1)}, bf16[64,128]{1,0:T(8,128)(2,1)S(1)}, u32[]{:S(2)}, u32[]{:S(2)}) collective-permute-start(bf16[64,128]{1,0:T(8,128)(2,1)S(1)} %slice_bitcast_fusion.3), channel_id=1, source_target_pairs={{0,4},{4,8},{8,12},{12,16},{16,20},{20,24},{24,28},{1,5},{5,9},{9,... | collective-permute-start | bytes 49160 | tf_op jit(solution)/shard_map/ppermute | solution.py:16
  19.7 0.8 copy.13
  20.6 3.5 %all-to-all-start.2 = ((bf16[256,4,128]{2,0,1:T(8,128)(2,1)}), bf16[256,4,128]{2,0,1:T(8,128)(2,1)S(1)}, u32[]{:S(2)}, u32[]{:S(2)}) async-start(bf16[256,4,128]{2,0,1:T(8,128)(2,1)} %copy.13), calls=%async_computation.2 | async-start | bytes 524288 | tf_op jit(solution)/shard_map/all_to_all | solution.py:76
  25.1 0.7 add_add_fusion
  26.0 0.8 copy.10
  26.9 3.2 %all-to-all-done.2 = bf16[256,4,128]{2,0,1:T(8,128)(2,1)S(1)} async-done(((bf16[256,4,128]{2,0,1:T(8,128)(2,1)}), bf16[256,4,128]{2,0,1:T(8,128)(2,1)S(1)}, u32[]{:S(2)}, u32[]{:S(2)}) %all-to-all-start.2) | async-done | bytes 262176 | tf_op jit(solution)/shard_map/all_to_all | solution.py:76
  30.1 3.4 %all-to-all-start = ((bf16[256,4,128]{2,0,1:T(8,128)(2,1)}), bf16[256,4,128]{2,0,1:T(8,128)(2,1)S(1)}, u32[]{:S(2)}, u32[]{:S(2)}) async-start(bf16[256,4,128]{2,0,1:T(8,128)(2,1)} %copy.10), calls=%async_computation | async-start | bytes 524288 | tf_op jit(solution)/shard_map/all_to_all | solution.py:75
  34.0 5.5 %all-to-all-done = bf16[256,4,128]{2,0,1:T(8,128)(2,1)S(1)} async-done(((bf16[256,4,128]{2,0,1:T(8,128)(2,1)}), bf16[256,4,128]{2,0,1:T(8,128)(2,1)S(1)}, u32[]{:S(2)}, u32[]{:S(2)}) %all-to-all-start) | async-done | bytes 262176 | tf_op jit(solution)/shard_map/all_to_all | solution.py:75
  40.7 1.3 %fusion.43 = f32[4,192,128]{2,1,0:T(8,128)} fusion(bf16[4,256,128]{2,1,0:T(8,128)(2,1)S(1)} %bitcast.71, f32[4,128]{1,0:T(4,128)S(1)} %get-tuple-element.74, bf16[4,256,128]{2,1,0:T(8,128)(2,1)S(1)} %bitcast.91, bf16[4,256,128]{2,1,0:T(8,128)(2,1)S(1)} %bitcast.83, bf16[3,64,128]{2,1,0:T(8,128)(2,1)S(1)} %slice.163, bf16[1,64,128]{2,1,0:T(8,128)(2,1)S(1)} %bitcast.105, ...), kind=kOutput, calls=%fused_computation.65 | convolution fusion | flops 53084864 | bytes 1040384 | tf_op jit(solution)/shard_map/dot_general | solution.py:60
  42.0 1.5 %fusion.103 = (f32[4,128]{1,0:T(4,128)S(1)}, f32[4,128,320]{1,2,0:T(8,128)}) fusion(bf16[4,256,128]{2,1,0:T(8,128)(2,1)S(1)} %bitcast.84, bf16[3,64,128]{2,1,0:T(8,128)(2,1)S(1)} %slice.163, bf16[1,64,128]{2,1,0:T(8,128)(2,1)S(1)} %bitcast.106, bf16[4,256,128]{2,1,0:T(8,128)(2,1)S(1)} %bitcast.92, pred[4]{0:T(512)(128)(4,1)S(1)} %add_compare_fusion, ...), kind=kOutput, calls=%fused_computation.111 | convolution fusion | flops 46367040 | bytes 1207296 | tf_op jit(solution)/shard_map/sub | solution.py:43
  43.6 0.9 %convolution_convert_fusion.2 = bf16[4,128,128]{2,1,0:T(8,128)(2,1)S(1)} fusion(bf16[4,256,128]{2,1,0:T(8,128)(2,1)S(1)} %bitcast.68, bf16[3,64,128]{2,1,0:T(8,128)(2,1)S(1)} %slice.166, bf16[1,64,128]{2,1,0:T(8,128)(2,1)S(1)} %bitcast.100, f32[4,128]{1,0:T(4,128)S(1)} %get-tuple-element.72, bf16[4,256,128]{2,1,0:T(8,128)(2,1)S(1)} %bitcast.85, ...), kind=kOutput, calls=%fused_computation.30 | convolution fusion | flops 89523008 | bytes 1010688 | tf_op jit(solution)/shard_map/dot_general | solution.py:46
  45.3 3.4 %all-to-all-start.1 = ((bf16[4,256,128]{2,1,0:T(8,128)(2,1)}), bf16[4,256,128]{2,1,0:T(8,128)(2,1)S(1)}, u32[]{:S(2)}, u32[]{:S(2)}) async-start(bf16[4,256,128]{2,1,0:T(8,128)(2,1)} %pad_maximum_fusion.4), calls=%async_computation.1 | async-start | bytes 524288 | tf_op jit(solution)/shard_map/all_to_all | solution.py:147
  48.7 1.7 %convolution_convert_fusion = bf16[4,128,128]{2,1,0:T(8,128)(2,1)S(1)} fusion(f32[4,128,320]{1,2,0:T(8,128)S(1)} %convolution_bitcast_fusion, bf16[4,256,128]{2,1,0:T(8,128)(2,1)S(1)} %bitcast.86, bf16[3,64,128]{2,1,0:T(8,128)(2,1)S(1)} %slice.163, bf16[1,64,128]{2,1,0:T(8,128)(2,1)S(1)} %bitcast.108, f32[4,128,320]{1,2,0:T(8,128)} %get-tuple-element.73, ...), kind=kOutput, calls=%fused_computation.28 | convolution fusion | flops 44139328 | bytes 1771520 | tf_op jit(solution)/shard_map/dot_general | solution.py:54
  50.4 1.0 %fusion.22 = f32[4,192,128]{2,1,0:T(8,128)} fusion(f32[4,128,192]{1,2,0:T(8,128)S(1)} %convolution_bitcast_fusion.1, bf16[4,256,128]{2,1,0:T(8,128)(2,1)S(1)} %bitcast.94, f32[4,128,192]{1,2,0:T(8,128)S(1)} %get-tuple-element.75, f32[4,128]{1,0:T(4,128)S(1)} %get-tuple-element.74), kind=kOutput, calls=%fused_computation.32 | convolution fusion | flops 25854656 | bytes 2101248 | tf_op jit(solution)/shard_map/dot_general | solution.py:57
  51.4 1.7 %convolution_add_fusion.1 = f32[4,320,128]{2,1,0:T(8,128)S(1)} fusion(f32[4,128,320]{1,2,0:T(8,128)S(1)} %convolution_bitcast_fusion, f32[4,192,128]{2,1,0:T(8,128)} %fusion.22, bf16[4,256,128]{2,1,0:T(8,128)(2,1)S(1)} %bitcast.95, f32[4,128,320]{1,2,0:T(8,128)} %get-tuple-element.73, f32[4,128]{1,0:T(4,128)S(1)} %get-tuple-element.72), kind=kOutput, calls=%fused_computation.11 | convolution fusion | flops 43254592 | bytes 3805184 | tf_op jit(solution)/shard_map/dot_general | solution.py:57
  53.2 3.3 %collective-permute-start.2 = (f32[64,128]{1,0:T(8,128)S(1)}, f32[64,128]{1,0:T(8,128)S(1)}, u32[]{:S(2)}, u32[]{:S(2)}) collective-permute-start(f32[64,128]{1,0:T(8,128)S(1)} %slice_bitcast_fusion.1), channel_id=1, source_target_pairs={{4,0},{8,4},{12,8},{16,12},{20,16},{24,20},{28,24},{5,1},{9,5},{13... | collective-permute-start | bytes 98312 | tf_op jit(solution)/shard_map/ppermute | solution.py:16
  56.6 1.9 %convolution_add_fusion = f32[4,320,128]{2,1,0:T(8,128)S(1)} fusion(f32[4,192,128]{2,1,0:T(8,128)} %fusion.43, bf16[4,256,128]{2,1,0:T(8,128)(2,1)S(1)} %bitcast.72, f32[4,128]{1,0:T(4,128)S(1)} %get-tuple-element.72, bf16[4,256,128]{2,1,0:T(8,128)(2,1)S(1)} %bitcast.87, bf16[3,64,128]{2,1,0:T(8,128)(2,1)S(1)} %copy-done.4, ...), kind=kOutput, calls=%fused_computation.10 | convolution fusion | flops 88638272 | bytes 1731584 | tf_op jit(solution)/shard_map/dot_general | solution.py:60
  59.6 3.4 %all-to-all-start.3 = ((bf16[4,256,128]{2,1,0:T(8,128)(2,1)}), bf16[4,256,128]{2,1,0:T(8,128)(2,1)S(1)}, u32[]{:S(2)}, u32[]{:S(2)}) async-start(bf16[4,256,128]{2,1,0:T(8,128)(2,1)} %pad_maximum_fusion.5), calls=%async_computation.3 | async-start | bytes 524288 | tf_op jit(solution)/shard_map/all_to_all | solution.py:148
  63.0 0.8 pad_maximum_fusion
  63.9 5.1 %all-to-all-done.3 = bf16[4,256,128]{2,1,0:T(8,128)(2,1)S(1)} async-done(((bf16[4,256,128]{2,1,0:T(8,128)(2,1)}), bf16[4,256,128]{2,1,0:T(8,128)(2,1)S(1)}, u32[]{:S(2)}, u32[]{:S(2)}) %all-to-all-start.3) | async-done | bytes 262176 | tf_op jit(solution)/shard_map/all_to_all | solution.py:148
  69.0 3.5 %all-to-all-start.4 = ((f32[4,256,128]{2,1,0:T(8,128)}), f32[4,256,128]{2,1,0:T(8,128)S(1)}, u32[]{:S(2)}, u32[]{:S(2)}) async-start(f32[4,256,128]{2,1,0:T(8,128)} %pad_maximum_fusion), calls=%async_computation.4 | async-start | bytes 1048576 | tf_op jit(solution)/shard_map/all_to_all | solution.py:151
  72.5 2.4 %collective-permute-start.3 = (f32[64,128]{1,0:T(8,128)S(1)}, f32[64,128]{1,0:T(8,128)S(1)}, u32[]{:S(2)}, u32[]{:S(2)}) collective-permute-start(f32[64,128]{1,0:T(8,128)S(1)} %slice_bitcast_fusion), channel_id=1, source_target_pairs={{4,0},{8,4},{12,8},{16,12},{20,16},{24,20},{28,24},{5,1},{9,5},{13... | collective-permute-start | bytes 98312 | tf_op jit(solution)/shard_map/ppermute | solution.py:16
  75.0 3.3 %collective-permute-done.3 = f32[64,128]{1,0:T(8,128)S(1)} collective-permute-done((f32[64,128]{1,0:T(8,128)S(1)}, f32[64,128]{1,0:T(8,128)S(1)}, u32[]{:S(2)}, u32[]{:S(2)}) %collective-permute-start.3) | collective-permute-done | bytes 32800 | tf_op jit(solution)/shard_map/ppermute | solution.py:16
  78.3 0.8 pad_maximum_fusion.1
  79.2 2.1 %all-to-all-done.4 = f32[4,256,128]{2,1,0:T(8,128)S(1)} async-done(((f32[4,256,128]{2,1,0:T(8,128)}), f32[4,256,128]{2,1,0:T(8,128)S(1)}, u32[]{:S(2)}, u32[]{:S(2)}) %all-to-all-start.4) | async-done | bytes 524320 | tf_op jit(solution)/shard_map/all_to_all | solution.py:151
  81.3 3.5 %all-to-all-start.5 = ((f32[4,256,128]{2,1,0:T(8,128)}), f32[4,256,128]{2,1,0:T(8,128)S(1)}, u32[]{:S(2)}, u32[]{:S(2)}) async-start(f32[4,256,128]{2,1,0:T(8,128)} %pad_maximum_fusion.1), calls=%async_computation.5 | async-start | bytes 1048576 | tf_op jit(solution)/shard_map/all_to_all | solution.py:152
  84.9 0.8 copy.15
  85.9 0.8 copy.16
  87.4 6.2 %all-to-all-done.5 = f32[4,256,128]{2,1,0:T(8,128)S(1)} async-done(((f32[4,256,128]{2,1,0:T(8,128)}), f32[4,256,128]{2,1,0:T(8,128)S(1)}, u32[]{:S(2)}, u32[]{:S(2)}) %all-to-all-start.5) | async-done | bytes 524320 | tf_op jit(solution)/shard_map/all_to_all | solution.py:152
  (65 shorter events, 6.4 us)
Async XLA Ops:
  0.6 9.7 %copy-start.2 = (bf16[256,128]{1,0:T(8,128)(2,1)S(1)}, bf16[256,128]{1,0:T(8,128)(2,1)}, u32[]{:S(2)}) copy-start(bf16[256,128]{1,0:T(8,128)(2,1)} %param.18) | copy-start | bytes 196612
  6.8 12.8 %copy-start = (bf16[256,512]{1,0:T(8,128)(2,1)S(1)}, bf16[256,512]{1,0:T(8,128)(2,1)}, u32[]{:S(2)}) copy-start(bf16[256,512]{1,0:T(8,128)(2,1)} %param.20) | copy-start | bytes 786436
  6.8 26.7 %collective-permute-start.1 = (bf16[64,128]{1,0:T(8,128)(2,1)S(1)}, bf16[64,128]{1,0:T(8,128)(2,1)S(1)}, u32[]{:S(2)}, u32[]{:S(2)}) collective-permute-start(bf16[64,128]{1,0:T(8,128)(2,1)S(1)} %slice_bitcast_fusion.2), channel_id=1, source_target_pairs={{0,4},{4,8},{8,12},{12,16},{16,20},{20,24},{24,28},{1,5},{5,9},{9,... | collective-permute-start | bytes 49160 | tf_op jit(solution)/shard_map/ppermute | solution.py:16
  16.1 17.9 %collective-permute-start = (bf16[64,128]{1,0:T(8,128)(2,1)S(1)}, bf16[64,128]{1,0:T(8,128)(2,1)S(1)}, u32[]{:S(2)}, u32[]{:S(2)}) collective-permute-start(bf16[64,128]{1,0:T(8,128)(2,1)S(1)} %slice_bitcast_fusion.3), channel_id=1, source_target_pairs={{0,4},{4,8},{8,12},{12,16},{16,20},{20,24},{24,28},{1,5},{5,9},{9,... | collective-permute-start | bytes 49160 | tf_op jit(solution)/shard_map/ppermute | solution.py:16
  20.5 3.7 %copy-start.8 = (s32[32]{0:T(128)S(1)}, s32[32]{0:T(128)}, u32[]{:S(2)}) copy-start(s32[32]{0:T(128)} %param.21) | copy-start | bytes 388
  20.6 9.5 %all-to-all-start.2 = ((bf16[256,4,128]{2,0,1:T(8,128)(2,1)}), bf16[256,4,128]{2,0,1:T(8,128)(2,1)S(1)}, u32[]{:S(2)}, u32[]{:S(2)}) async-start(bf16[256,4,128]{2,0,1:T(8,128)(2,1)} %copy.13), calls=%async_computation.2 | async-start | bytes 524288 | tf_op jit(solution)/shard_map/all_to_all | solution.py:76
  24.1 1.8 %copy-start.1 = (bf16[256,512]{1,0:T(8,128)(2,1)S(1)}, bf16[256,512]{1,0:T(8,128)(2,1)}, u32[]{:S(2)}) copy-start(bf16[256,512]{1,0:T(8,128)(2,1)} %param.17) | copy-start | bytes 786436
  24.1 19.4 %copy-start.11 = (pred[320]{0:T(512)(128)(4,1)}, pred[320]{0:T(512)(128)(4,1)S(1)}, u32[]{:S(2)}) copy-start(pred[320]{0:T(512)(128)(4,1)S(1)} %broadcast_compare_fusion.1) | copy-start | bytes 964
  24.2 19.4 %copy-start.9 = (pred[4]{0:T(512)(128)(4,1)}, pred[4]{0:T(512)(128)(4,1)S(1)}, u32[]{:S(2)}) copy-start(pred[4]{0:T(512)(128)(4,1)S(1)} %add_compare_fusion) | copy-start | bytes 16
  25.1 18.5 %copy-start.5 = (pred[128,320]{0,1:T(8,128)(4,1)}, pred[128,320]{0,1:T(8,128)(4,1)S(1)}, u32[]{:S(2)}) copy-start(pred[128,320]{0,1:T(8,128)(4,1)S(1)} %broadcast_compare_fusion) | copy-start | bytes 122884
  25.9 22.8 %copy-start.3 = (bf16[3,64,128]{2,1,0:T(8,128)(2,1)}, bf16[3,64,128]{2,1,0:T(8,128)(2,1)S(1)}, u32[]{:S(2)}) copy-start(bf16[3,64,128]{2,1,0:T(8,128)(2,1)S(1)} %slice.163) | copy-start | bytes 147460
  30.1 9.4 %all-to-all-start = ((bf16[256,4,128]{2,0,1:T(8,128)(2,1)}), bf16[256,4,128]{2,0,1:T(8,128)(2,1)S(1)}, u32[]{:S(2)}, u32[]{:S(2)}) async-start(bf16[256,4,128]{2,0,1:T(8,128)(2,1)} %copy.10), calls=%async_computation | async-start | bytes 524288 | tf_op jit(solution)/shard_map/all_to_all | solution.py:75
  34.0 14.7 %copy-start.6 = (bf16[64,128]{1,0:T(8,128)(2,1)}, bf16[64,128]{1,0:T(8,128)(2,1)S(1)}, u32[]{:S(2)}) copy-start(bf16[64,128]{1,0:T(8,128)(2,1)S(1)} %collective-permute-done) | copy-start | bytes 49156
  45.3 14.3 %all-to-all-start.1 = ((bf16[4,256,128]{2,1,0:T(8,128)(2,1)}), bf16[4,256,128]{2,1,0:T(8,128)(2,1)S(1)}, u32[]{:S(2)}, u32[]{:S(2)}) async-start(bf16[4,256,128]{2,1,0:T(8,128)(2,1)} %pad_maximum_fusion.4), calls=%async_computation.1 | async-start | bytes 524288 | tf_op jit(solution)/shard_map/all_to_all | solution.py:147
  51.4 5.1 %copy-start.10 = (pred[4]{0:T(512)(128)(4,1)S(1)}, pred[4]{0:T(512)(128)(4,1)}, u32[]{:S(2)}) copy-start(pred[4]{0:T(512)(128)(4,1)} %copy-done.9) | copy-start | bytes 16
  51.4 5.1 %copy-start.12 = (pred[320]{0:T(512)(128)(4,1)S(1)}, pred[320]{0:T(512)(128)(4,1)}, u32[]{:S(2)}) copy-start(pred[320]{0:T(512)(128)(4,1)} %copy-done.11) | copy-start | bytes 964
  53.2 3.4 %copy-start.4 = (bf16[3,64,128]{2,1,0:T(8,128)(2,1)S(1)}, bf16[3,64,128]{2,1,0:T(8,128)(2,1)}, u32[]{:S(2)}) copy-start(bf16[3,64,128]{2,1,0:T(8,128)(2,1)} %copy-done.3) | copy-start | bytes 147460
  53.2 3.4 %copy-start.7 = (bf16[64,128]{1,0:T(8,128)(2,1)S(1)}, bf16[64,128]{1,0:T(8,128)(2,1)}, u32[]{:S(2)}) copy-start(bf16[64,128]{1,0:T(8,128)(2,1)} %copy-done.6) | copy-start | bytes 49156
  53.2 9.8 %collective-permute-start.2 = (f32[64,128]{1,0:T(8,128)S(1)}, f32[64,128]{1,0:T(8,128)S(1)}, u32[]{:S(2)}, u32[]{:S(2)}) collective-permute-start(f32[64,128]{1,0:T(8,128)S(1)} %slice_bitcast_fusion.1), channel_id=1, source_target_pairs={{4,0},{8,4},{12,8},{16,12},{20,16},{24,20},{28,24},{5,1},{9,5},{13... | collective-permute-start | bytes 98312 | tf_op jit(solution)/shard_map/ppermute | solution.py:16
  59.6 9.4 %all-to-all-start.3 = ((bf16[4,256,128]{2,1,0:T(8,128)(2,1)}), bf16[4,256,128]{2,1,0:T(8,128)(2,1)S(1)}, u32[]{:S(2)}, u32[]{:S(2)}) async-start(bf16[4,256,128]{2,1,0:T(8,128)(2,1)} %pad_maximum_fusion.5), calls=%async_computation.3 | async-start | bytes 524288 | tf_op jit(solution)/shard_map/all_to_all | solution.py:148
  69.0 12.3 %all-to-all-start.4 = ((f32[4,256,128]{2,1,0:T(8,128)}), f32[4,256,128]{2,1,0:T(8,128)S(1)}, u32[]{:S(2)}, u32[]{:S(2)}) async-start(f32[4,256,128]{2,1,0:T(8,128)} %pad_maximum_fusion), calls=%async_computation.4 | async-start | bytes 1048576 | tf_op jit(solution)/shard_map/all_to_all | solution.py:151
  72.5 5.8 %collective-permute-start.3 = (f32[64,128]{1,0:T(8,128)S(1)}, f32[64,128]{1,0:T(8,128)S(1)}, u32[]{:S(2)}, u32[]{:S(2)}) collective-permute-start(f32[64,128]{1,0:T(8,128)S(1)} %slice_bitcast_fusion), channel_id=1, source_target_pairs={{4,0},{8,4},{12,8},{16,12},{20,16},{24,20},{28,24},{5,1},{9,5},{13... | collective-permute-start | bytes 98312 | tf_op jit(solution)/shard_map/ppermute | solution.py:16
  81.3 12.3 %all-to-all-start.5 = ((f32[4,256,128]{2,1,0:T(8,128)}), f32[4,256,128]{2,1,0:T(8,128)S(1)}, u32[]{:S(2)}, u32[]{:S(2)}) async-start(f32[4,256,128]{2,1,0:T(8,128)} %pad_maximum_fusion.1), calls=%async_computation.5 | async-start | bytes 1048576 | tf_op jit(solution)/shard_map/all_to_all | solution.py:152
where the time goes:
time: 95.1 us; the launch traced here: 94.2 us
  starting transfers between devices  33.4 us (35%)
  waiting for transfers between devices  25.5 us (27%)
  matrix products  12.1 us (13%)
  blocking collectives  11.9 us (13%)
  other arithmetic  5.42 us (6%)
  local copies, waits for them, and re-layouts  4.74 us (5%)
  between operations  1.09 us (1%)
    ppermute x4, starting transfers between devices, passed_along(): lax.ppermute(value, axis, [(source, source + steps) for source in range(f...  12.7 us
    all_to_all x1, waiting for transfers between devices, per_device(): lax.all_to_all(own_v, 'head', split_axis=0, concat_axis=1, tiled=True)  6.16 us
    all_gather x1, blocking collectives, per_device(): lax.all_gather(value_rows, 'head', axis=0, tiled=True)  6.13 us
    all_gather x1, blocking collectives, per_device(): lax.all_gather(key_rows, 'head', axis=0, tiled=True)  5.79 us
    all_to_all x1, waiting for transfers between devices, per_device(): lax.all_to_all(queries, 'head', split_axis=1, concat_axis=0, tiled=True)  5.5 us
    all_to_all x1, waiting for transfers between devices, per_device(): lax.all_to_all(all_query_grads, 'head', split_axis=0, concat_axis=1, tile...  5.14 us
    all_to_all x1, starting transfers between devices, per_device(): lax.all_to_all(out_grad, 'head', split_axis=1, concat_axis=0, tiled=True)  3.54 us
    all_to_all x1, starting transfers between devices, per_device(): lax.all_to_all(own_v, 'head', split_axis=0, concat_axis=1, tiled=True)  3.47 us
  transfers between devices with their start and end apart: 10, of which 6 were waited for; matrix products, arithmetic and copies ran while one was open for 17% of the time, Pallas kernels for 0%

commit v1 on v0

--- a/solution.py
+++ b/solution.py
@@ -8,6 +8,22 @@
 GROUP = 4
 SPANS_DEV = 4
 masked_fill = -1e30
+
+
+def exchange_in_pairs(x, axis, split, join):
+    ways, here = (lax.axis_size(axis), lax.axis_index(axis))
+    width = x.shape[split] // ways
+    shape = list(x.shape)
+    shape[split] = width
+    height = shape[join]
+    shape[join] = height * ways
+    full = jnp.zeros(shape, x.dtype)
+    for mask in range(ways):
+        part = lax.dynamic_slice_in_dim(x, (here ^ mask) * width, width, axis=split)
+        if mask:
+            part = lax.ppermute(part, axis, [(d, d ^ mask) for d in range(ways)])
+        full = lax.dynamic_update_slice_in_dim(full, part, (here ^ mask) * height, axis=join)
+    return full
 
 
 def passed_along(value, axis, steps):
@@ -144,7 +160,7 @@
     all_results = jnp.concatenate(results, axis=1).reshape(group_rows, HD)
     all_query_grads = jnp.concatenate(query_grads, axis=1).reshape(group_rows, HD)
     outputs, query_grad = (
-        lax.all_to_all(all_results, "head", split_axis=0, concat_axis=1, tiled=True),
+        exchange_in_pairs(all_results, "head", 0, 1),
         lax.all_to_all(all_query_grads, "head", split_axis=0, concat_axis=1, tiled=True),
     )
     wide_gk, wide_gv = (

time: 95.1 us -> 90 us (0.946)
  matrix products: 12.1 us -> 9.09 us
    ppermute x0 -> x3, waiting for transfers between devices: none -> 9.11 us  [exchange_in_pairs(): part = lax.ppermute(part, axis, [(d, d ^ mask) for d in range(ways)])]
    all_to_all x1, waiting for transfers between devices: 6.16 us -> 0.01 us  [per_device(): lax.all_to_all(own_v, 'head', split_axis=0, concat_axis=1, tiled=True)]
    all_to_all x1, waiting for transfers between devices: 2.12 us -> 7.28 us  [per_device(): lax.all_to_all(own_k, 'head', split_axis=0, concat_axis=1, tiled=True)]
    all_to_all x1, waiting for transfers between devices: 5.14 us -> 0.01 us  [per_device(): lax.all_to_all(all_query_grads, 'head', split_axis=0, concat_axis=1, tile...]
    all_to_all x1 -> x0, starting transfers between devices: 3.41 us -> none  [per_device(): lax.all_to_all(all_results, 'head', split_axis=0, concat_axis=1, tiled=True)]
    ppermute x4, waiting for transfers between devices: 3.34 us -> 0.01 us  [passed_along(): lax.ppermute(value, axis, [(source, source + steps) for source in range(f...]
    ppermute x0 -> x3, starting transfers between devices: none -> 2.5 us  [exchange_in_pairs(): part = lax.ppermute(part, axis, [(d, d ^ mask) for d in range(ways)])]
    dot_general x2, matrix products: 2.07 us -> 0.76 us  [attend(): lax.dot_general(grad_scores, key_block, forward, preferred_element_type=j...]
  transfers between devices with their start and end apart: 10 -> 12, of which waited for: 6 -> 5; matrix products, arithmetic and copies ran while one was open for 17% -> 12% of each run, Pallas kernels for 0% -> 0%
where the time goes in v1:
time: 90 us; the launch traced here: 88.8 us
  starting transfers between devices  32.5 us (36%)
  waiting for transfers between devices  25.2 us (28%)
  blocking collectives  11.9 us (13%)
  matrix products  9.09 us (10%)
  other arithmetic  4.72 us (5%)
  local copies, waits for them, and re-layouts  4.37 us (5%)
  between operations  1.06 us (1%)
    ppermute x4, starting transfers between devices, passed_along(): lax.ppermute(value, axis, [(source, source + steps) for source in range(f...  12.7 us
    ppermute x3, waiting for transfers between devices, exchange_in_pairs(): part = lax.ppermute(part, axis, [(d, d ^ mask) for d in range(ways)])  9.11 us
    all_to_all x1, waiting for transfers between devices, per_device(): lax.all_to_all(own_k, 'head', split_axis=0, concat_axis=1, tiled=True)  7.28 us
    all_gather x1, blocking collectives, per_device(): lax.all_gather(value_rows, 'head', axis=0, tiled=True)  6.13 us
    all_gather x1, blocking collectives, per_device(): lax.all_gather(key_rows, 'head', axis=0, tiled=True)  5.79 us
    all_to_all x1, waiting for transfers between devices, per_device(): lax.all_to_all(queries, 'head', split_axis=1, concat_axis=0, tiled=True)  5.51 us
    all_to_all x1, starting transfers between devices, per_device(): lax.all_to_all(out_grad, 'head', split_axis=1, concat_axis=0, tiled=True)  3.54 us
    all_to_all x1, starting transfers between devices, per_device(): lax.all_to_all(own_k, 'head', split_axis=0, concat_axis=1, tiled=True)  3.47 us
  transfers between devices with their start and end apart: 12, of which 5 were waited for; matrix products, arithmetic and copies ran while one was open for 12% of the time, Pallas kernels for 0%

profile of v1, /device:TPU:8, one launch (start us, length us, event | category | flops | bytes accessed | tf_op | source)
XLA Modules:
  0.0 88.8 jit_solution(10593506448366864819)
XLA Ops:
  0.6 6.1 %all_gather.7 = bf16[1024,128]{1,0:T(8,128)(2,1)S(1)} all-gather(bf16[256,128]{1,0:T(8,128)(2,1)} %param.19), channel_id=1, replica_groups=mesh['seq'=8,'head'=4] {'head'}, dimensions={0}, use_global_device_ids=true | all-gather | bytes 327680 | tf_op jit(solution)/shard_map/all_gather | solution.py:96
  6.8 3.5 %collective-permute-start.1 = (bf16[64,128]{1,0:T(8,128)(2,1)S(1)}, bf16[64,128]{1,0:T(8,128)(2,1)S(1)}, u32[]{:S(2)}, u32[]{:S(2)}) collective-permute-start(bf16[64,128]{1,0:T(8,128)(2,1)S(1)} %slice_bitcast_fusion.2), channel_id=1, source_target_pairs={{0,4},{4,8},{8,12},{12,16},{16,20},{20,24},{24,28},{1,5},{5,9},{9,... | collective-permute-start | bytes 49160 | tf_op jit(solution)/shard_map/ppermute | solution.py:32
  10.3 5.8 %all_gather.6 = bf16[1024,128]{1,0:T(8,128)(2,1)S(1)} all-gather(bf16[256,128]{1,0:T(8,128)(2,1)S(1)} %copy-done.3), channel_id=1, replica_groups=mesh['seq'=8,'head'=4] {'head'}, dimensions={0}, use_global_device_ids=true | all-gather | bytes 327680 | tf_op jit(solution)/shard_map/all_gather | solution.py:95
  16.1 3.4 %collective-permute-start = (bf16[64,128]{1,0:T(8,128)(2,1)S(1)}, bf16[64,128]{1,0:T(8,128)(2,1)S(1)}, u32[]{:S(2)}, u32[]{:S(2)}) collective-permute-start(bf16[64,128]{1,0:T(8,128)(2,1)S(1)} %slice_bitcast_fusion.3), channel_id=1, source_target_pairs={{0,4},{4,8},{8,12},{12,16},{16,20},{20,24},{24,28},{1,5},{5,9},{9,... | collective-permute-start | bytes 49160 | tf_op jit(solution)/shard_map/ppermute | solution.py:32
  19.7 0.8 copy.12
  20.6 3.5 %all-to-all-start.1 = ((bf16[256,4,128]{2,0,1:T(8,128)(2,1)}), bf16[256,4,128]{2,0,1:T(8,128)(2,1)S(1)}, u32[]{:S(2)}, u32[]{:S(2)}) async-start(bf16[256,4,128]{2,0,1:T(8,128)(2,1)} %copy.12), calls=%async_computation.1 | async-start | bytes 524288 | tf_op jit(solution)/shard_map/all_to_all | solution.py:92
  24.3 0.6 dynamic_slice.21
  25.1 0.7 add_add_fusion
  26.0 0.8 copy.10
  26.8 3.3 %all-to-all-done.1 = bf16[256,4,128]{2,0,1:T(8,128)(2,1)S(1)} async-done(((bf16[256,4,128]{2,0,1:T(8,128)(2,1)}), bf16[256,4,128]{2,0,1:T(8,128)(2,1)S(1)}, u32[]{:S(2)}, u32[]{:S(2)}) %all-to-all-start.1) | async-done | bytes 262176 | tf_op jit(solution)/shard_map/all_to_all | solution.py:92
  30.1 3.4 %all-to-all-start = ((bf16[256,4,128]{2,0,1:T(8,128)(2,1)}), bf16[256,4,128]{2,0,1:T(8,128)(2,1)S(1)}, u32[]{:S(2)}, u32[]{:S(2)}) async-start(bf16[256,4,128]{2,0,1:T(8,128)(2,1)} %copy.10), calls=%async_computation | async-start | bytes 524288 | tf_op jit(solution)/shard_map/all_to_all | solution.py:91
  34.0 5.5 %all-to-all-done = bf16[256,4,128]{2,0,1:T(8,128)(2,1)S(1)} async-done(((bf16[256,4,128]{2,0,1:T(8,128)(2,1)}), bf16[256,4,128]{2,0,1:T(8,128)(2,1)S(1)}, u32[]{:S(2)}, u32[]{:S(2)}) %all-to-all-start) | async-done | bytes 262176 | tf_op jit(solution)/shard_map/all_to_all | solution.py:91
  40.0 0.7 convolution_convert_fusion.3
  41.3 1.3 %fusion.43 = f32[4,192,128]{2,1,0:T(8,128)} fusion(bf16[4,256,128]{2,1,0:T(8,128)(2,1)S(1)} %bitcast.71, f32[4,128]{1,0:T(4,128)S(1)} %get-tuple-element.78, bf16[4,256,128]{2,1,0:T(8,128)(2,1)S(1)} %bitcast.90, bf16[4,256,128]{2,1,0:T(8,128)(2,1)S(1)} %bitcast.82, bf16[3,64,128]{2,1,0:T(8,128)(2,1)S(1)} %slice.163, bf16[1,64,128]{2,1,0:T(8,128)(2,1)S(1)} %bitcast.104, ...), kind=kOutput, calls=%fused_computation.65 | convolution fusion | flops 53084864 | bytes 1040384 | tf_op jit(solution)/shard_map/dot_general | solution.py:76
  42.6 0.7 fusion.103
  43.3 0.9 %convolution_convert_fusion.2 = bf16[4,128,128]{2,1,0:T(8,128)(2,1)S(1)} fusion(bf16[4,256,128]{2,1,0:T(8,128)(2,1)S(1)} %bitcast.67, bf16[3,64,128]{2,1,0:T(8,128)(2,1)S(1)} %slice.166, bf16[1,64,128]{2,1,0:T(8,128)(2,1)S(1)} %bitcast.98, f32[4,128]{1,0:T(4,128)S(1)} %get-tuple-element.76, bf16[4,256,128]{2,1,0:T(8,128)(2,1)S(1)} %bitcast.84, ...), kind=kOutput, calls=%fused_computation.30 | convolution fusion | flops 89523008 | bytes 1010688 | tf_op jit(solution)/shard_map/dot_general | solution.py:62
  44.7 0.7 pad_maximum_fusion.5
  45.4 3.4 %all-to-all-start.2 = ((bf16[4,256,128]{2,1,0:T(8,128)(2,1)}), bf16[4,256,128]{2,1,0:T(8,128)(2,1)S(1)}, u32[]{:S(2)}, u32[]{:S(2)}) async-start(bf16[4,256,128]{2,1,0:T(8,128)(2,1)} %pad_maximum_fusion.5), calls=%async_computation.2 | async-start | bytes 524288 | tf_op jit(solution)/shard_map/all_to_all | solution.py:164
  48.9 1.6 %convolution_add_fusion.1 = f32[4,320,128]{2,1,0:T(8,128)S(1)} fusion(f32[4,128,320]{1,2,0:T(8,128)S(1)} %convolution_bitcast_fusion, f32[4,192,128]{2,1,0:T(8,128)S(1)} %fusion.22, bf16[4,256,128]{2,1,0:T(8,128)(2,1)S(1)} %bitcast.93, f32[4,128,320]{1,2,0:T(8,128)} %copy-done.5, f32[4,128]{1,0:T(4,128)S(1)} %get-tuple-element.76), kind=kOutput, calls=%fused_computation.11 | convolution fusion | flops 43254592 | bytes 3805184 | tf_op jit(solution)/shard_map/dot_general | solution.py:73
  50.5 3.3 %collective-permute-start.5 = (f32[64,128]{1,0:T(8,128)S(1)}, f32[64,128]{1,0:T(8,128)S(1)}, u32[]{:S(2)}, u32[]{:S(2)}) collective-permute-start(f32[64,128]{1,0:T(8,128)S(1)} %slice_bitcast_fusion.1), channel_id=1, source_target_pairs={{4,0},{8,4},{12,8},{16,12},{20,16},{24,20},{28,24},{5,1},{9,5},{13... | collective-permute-start | bytes 98312 | tf_op jit(solution)/shard_map/ppermute | solution.py:32
  53.8 1.8 %convolution_add_fusion = f32[4,320,128]{2,1,0:T(8,128)S(1)} fusion(f32[4,192,128]{2,1,0:T(8,128)} %fusion.43, bf16[4,256,128]{2,1,0:T(8,128)(2,1)S(1)} %bitcast.72, f32[4,128]{1,0:T(4,128)S(1)} %get-tuple-element.76, bf16[4,256,128]{2,1,0:T(8,128)(2,1)S(1)} %bitcast.86, bf16[3,64,128]{2,1,0:T(8,128)(2,1)S(1)} %slice.163, ...), kind=kOutput, calls=%fused_computation.10 | convolution fusion | flops 88638272 | bytes 1731584 | tf_op jit(solution)/shard_map/dot_general | solution.py:76
  55.7 2.4 %collective-permute-start.6 = (f32[64,128]{1,0:T(8,128)S(1)}, f32[64,128]{1,0:T(8,128)S(1)}, u32[]{:S(2)}, u32[]{:S(2)}) collective-permute-start(f32[64,128]{1,0:T(8,128)S(1)} %slice_bitcast_fusion), channel_id=1, source_target_pairs={{4,0},{8,4},{12,8},{16,12},{20,16},{24,20},{28,24},{5,1},{9,5},{13... | collective-permute-start | bytes 98312 | tf_op jit(solution)/shard_map/ppermute | solution.py:32
  58.2 0.8 pad_maximum_fusion
  59.0 3.5 %all-to-all-start.3 = ((f32[4,256,128]{2,1,0:T(8,128)}), f32[4,256,128]{2,1,0:T(8,128)S(1)}, u32[]{:S(2)}, u32[]{:S(2)}) async-start(f32[4,256,128]{2,1,0:T(8,128)} %pad_maximum_fusion), calls=%async_computation.3 | async-start | bytes 1048576 | tf_op jit(solution)/shard_map/all_to_all | solution.py:167
  63.2 0.8 pad_maximum_fusion.1
  64.0 7.3 %all-to-all-done.3 = f32[4,256,128]{2,1,0:T(8,128)S(1)} async-done(((f32[4,256,128]{2,1,0:T(8,128)}), f32[4,256,128]{2,1,0:T(8,128)S(1)}, u32[]{:S(2)}, u32[]{:S(2)}) %all-to-all-start.3) | async-done | bytes 524320 | tf_op jit(solution)/shard_map/all_to_all | solution.py:167
  71.3 3.5 %all-to-all-start.4 = ((f32[4,256,128]{2,1,0:T(8,128)}), f32[4,256,128]{2,1,0:T(8,128)S(1)}, u32[]{:S(2)}, u32[]{:S(2)}) async-start(f32[4,256,128]{2,1,0:T(8,128)} %pad_maximum_fusion.1), calls=%async_computation.4 | async-start | bytes 1048576 | tf_op jit(solution)/shard_map/all_to_all | solution.py:168
  74.8 2.0 %collective-permute-start.3 = (bf16[256,128]{1,0:T(8,128)(2,1)S(1)}, bf16[256,128]{1,0:T(8,128)(2,1)S(1)}, u32[]{:S(2)}, u32[]{:S(2)}) collective-permute-start(bf16[256,128]{1,0:T(8,128)(2,1)S(1)} %get-tuple-element.73), channel_id=1, source_target_pairs={{0,2},{1,3},{2,0},{3,1},{4,6},{5,7},{6,4},{7,5},{8,10},{9,11},{10,... | collective-permute-start | bytes 196616 | tf_op jit(solution)/shard_map/ppermute | solution.py:24
  76.8 8.7 %collective-permute-done.3 = bf16[256,128]{1,0:T(8,128)(2,1)S(1)} collective-permute-done((bf16[256,128]{1,0:T(8,128)(2,1)S(1)}, bf16[256,128]{1,0:T(8,128)(2,1)S(1)}, u32[]{:S(2)}, u32[]{:S(2)}) %collective-permute-start.3) | collective-permute-done | bytes 65568 | tf_op jit(solution)/shard_map/ppermute | solution.py:24
  86.7 0.8 copy.14
  87.5 0.7 reduce_sum.58
  88.2 0.7 reduce_sum.59
  (58 shorter events, 4.5 us)
Async XLA Ops:
  0.6 9.7 %copy-start.3 = (bf16[256,128]{1,0:T(8,128)(2,1)S(1)}, bf16[256,128]{1,0:T(8,128)(2,1)}, u32[]{:S(2)}) copy-start(bf16[256,128]{1,0:T(8,128)(2,1)} %param.18) | copy-start | bytes 196612
  6.8 12.8 %copy-start = (bf16[256,512]{1,0:T(8,128)(2,1)S(1)}, bf16[256,512]{1,0:T(8,128)(2,1)}, u32[]{:S(2)}) copy-start(bf16[256,512]{1,0:T(8,128)(2,1)} %param.20) | copy-start | bytes 786436
  6.8 26.7 %collective-permute-start.1 = (bf16[64,128]{1,0:T(8,128)(2,1)S(1)}, bf16[64,128]{1,0:T(8,128)(2,1)S(1)}, u32[]{:S(2)}, u32[]{:S(2)}) collective-permute-start(bf16[64,128]{1,0:T(8,128)(2,1)S(1)} %slice_bitcast_fusion.2), channel_id=1, source_target_pairs={{0,4},{4,8},{8,12},{12,16},{16,20},{20,24},{24,28},{1,5},{5,9},{9,... | collective-permute-start | bytes 49160 | tf_op jit(solution)/shard_map/ppermute | solution.py:32
  16.1 17.9 %collective-permute-start = (bf16[64,128]{1,0:T(8,128)(2,1)S(1)}, bf16[64,128]{1,0:T(8,128)(2,1)S(1)}, u32[]{:S(2)}, u32[]{:S(2)}) collective-permute-start(bf16[64,128]{1,0:T(8,128)(2,1)S(1)} %slice_bitcast_fusion.3), channel_id=1, source_target_pairs={{0,4},{4,8},{8,12},{12,16},{16,20},{20,24},{24,28},{1,5},{5,9},{9,... | collective-permute-start | bytes 49160 | tf_op jit(solution)/shard_map/ppermute | solution.py:32
  20.5 3.6 %copy-start.4 = (s32[32]{0:T(128)S(1)}, s32[32]{0:T(128)}, u32[]{:S(2)}) copy-start(s32[32]{0:T(128)} %param.21) | copy-start | bytes 388
  20.6 9.5 %all-to-all-start.1 = ((bf16[256,4,128]{2,0,1:T(8,128)(2,1)}), bf16[256,4,128]{2,0,1:T(8,128)(2,1)S(1)}, u32[]{:S(2)}, u32[]{:S(2)}) async-start(bf16[256,4,128]{2,0,1:T(8,128)(2,1)} %copy.12), calls=%async_computation.1 | async-start | bytes 524288 | tf_op jit(solution)/shard_map/all_to_all | solution.py:92
  24.1 1.7 %copy-start.1 = (bf16[256,512]{1,0:T(8,128)(2,1)S(1)}, bf16[256,512]{1,0:T(8,128)(2,1)}, u32[]{:S(2)}) copy-start(bf16[256,512]{1,0:T(8,128)(2,1)} %param.17) | copy-start | bytes 786436
  30.1 9.4 %all-to-all-start = ((bf16[256,4,128]{2,0,1:T(8,128)(2,1)}), bf16[256,4,128]{2,0,1:T(8,128)(2,1)S(1)}, u32[]{:S(2)}, u32[]{:S(2)}) async-start(bf16[256,4,128]{2,0,1:T(8,128)(2,1)} %copy.10), calls=%async_computation | async-start | bytes 524288 | tf_op jit(solution)/shard_map/all_to_all | solution.py:91
  43.3 1.0 %copy-start.5 = (f32[4,128,320]{1,2,0:T(8,128)}, f32[4,128,320]{1,2,0:T(8,128)S(1)}, u32[]{:S(2)}) copy-start(f32[4,128,320]{1,2,0:T(8,128)S(1)} %get-tuple-element.77) | copy-start | bytes 1966084
  45.4 13.6 %all-to-all-start.2 = ((bf16[4,256,128]{2,1,0:T(8,128)(2,1)}), bf16[4,256,128]{2,1,0:T(8,128)(2,1)S(1)}, u32[]{:S(2)}, u32[]{:S(2)}) async-start(bf16[4,256,128]{2,1,0:T(8,128)(2,1)} %pad_maximum_fusion.5), calls=%async_computation.2 | async-start | bytes 524288 | tf_op jit(solution)/shard_map/all_to_all | solution.py:164
  50.5 7.7 %collective-permute-start.5 = (f32[64,128]{1,0:T(8,128)S(1)}, f32[64,128]{1,0:T(8,128)S(1)}, u32[]{:S(2)}, u32[]{:S(2)}) collective-permute-start(f32[64,128]{1,0:T(8,128)S(1)} %slice_bitcast_fusion.1), channel_id=1, source_target_pairs={{4,0},{8,4},{12,8},{16,12},{20,16},{24,20},{28,24},{5,1},{9,5},{13... | collective-permute-start | bytes 98312 | tf_op jit(solution)/shard_map/ppermute | solution.py:32
  55.7 7.5 %collective-permute-start.6 = (f32[64,128]{1,0:T(8,128)S(1)}, f32[64,128]{1,0:T(8,128)S(1)}, u32[]{:S(2)}, u32[]{:S(2)}) collective-permute-start(f32[64,128]{1,0:T(8,128)S(1)} %slice_bitcast_fusion), channel_id=1, source_target_pairs={{4,0},{8,4},{12,8},{16,12},{20,16},{24,20},{28,24},{5,1},{9,5},{13... | collective-permute-start | bytes 98312 | tf_op jit(solution)/shard_map/ppermute | solution.py:32
  59.0 12.3 %all-to-all-start.3 = ((f32[4,256,128]{2,1,0:T(8,128)}), f32[4,256,128]{2,1,0:T(8,128)S(1)}, u32[]{:S(2)}, u32[]{:S(2)}) async-start(f32[4,256,128]{2,1,0:T(8,128)} %pad_maximum_fusion), calls=%async_computation.3 | async-start | bytes 1048576 | tf_op jit(solution)/shard_map/all_to_all | solution.py:167
  62.6 14.2 %collective-permute-start.2 = (bf16[256,128]{1,0:T(8,128)(2,1)S(1)}, bf16[256,128]{1,0:T(8,128)(2,1)S(1)}, u32[]{:S(2)}, u32[]{:S(2)}) collective-permute-start(bf16[256,128]{1,0:T(8,128)(2,1)S(1)} %get-tuple-element.74), channel_id=1, source_target_pairs={{0,1},{1,0},{2,3},{3,2},{4,5},{5,4},{6,7},{7,6},{8,9},{9,8},{10,11... | collective-permute-start | bytes 196616 | tf_op jit(solution)/shard_map/ppermute | solution.py:24
  71.3 16.9 %all-to-all-start.4 = ((f32[4,256,128]{2,1,0:T(8,128)}), f32[4,256,128]{2,1,0:T(8,128)S(1)}, u32[]{:S(2)}, u32[]{:S(2)}) async-start(f32[4,256,128]{2,1,0:T(8,128)} %pad_maximum_fusion.1), calls=%async_computation.4 | async-start | bytes 1048576 | tf_op jit(solution)/shard_map/all_to_all | solution.py:168
  74.8 10.7 %collective-permute-start.3 = (bf16[256,128]{1,0:T(8,128)(2,1)S(1)}, bf16[256,128]{1,0:T(8,128)(2,1)S(1)}, u32[]{:S(2)}, u32[]{:S(2)}) collective-permute-start(bf16[256,128]{1,0:T(8,128)(2,1)S(1)} %get-tuple-element.73), channel_id=1, source_target_pairs={{0,2},{1,3},{2,0},{3,1},{4,6},{5,7},{6,4},{7,5},{8,10},{9,11},{10,... | collective-permute-start | bytes 196616 | tf_op jit(solution)/shard_map/ppermute | solution.py:24
  76.8 9.2 %collective-permute-start.4 = (bf16[256,128]{1,0:T(8,128)(2,1)S(1)}, bf16[256,128]{1,0:T(8,128)(2,1)S(1)}, u32[]{:S(2)}, u32[]{:S(2)}) collective-permute-start(bf16[256,128]{1,0:T(8,128)(2,1)S(1)} %get-tuple-element.72), channel_id=1, source_target_pairs={{0,3},{1,2},{2,1},{3,0},{4,7},{5,6},{6,5},{7,4},{8,11},{9,10},{10,... | collective-permute-start | bytes 196616 | tf_op jit(solution)/shard_map/ppermute | solution.py:24
  86.0 0.7 copy-start.2
